TPU v7x, 32 devices: a whole 2x2x4 slice. The times are simulated.
32 devices in a mesh: adapter: 8 (over z, x), feature: 4 (over y, core).
Axes of the slice: x: 2, y: 2, z: 4, core: 2. Of those that a mesh axis runs over, the one named last changes fastest.
Arguments:
- adapter_down: bfloat16 [128, 16, 8192], P('adapter', None, 'feature'), may hold values from -6 to 6
- adapter_up: bfloat16 [128, 16, 8192], P('adapter', None, 'feature'), may hold values from -6 to 6
- fisher: float32 [128], P('adapter'), may hold values from 0.1 to 10
- init_v: float32 [8192, 64], P('feature'), may hold values from -0.0625 to 0.0625
- init_u: float32 [8192, 64], P('feature'), may hold values from -0.0625 to 0.0625
- prompt_rows: bfloat16 [4096, 8192], P('adapter', 'feature'), may hold values from -6 to 6
- request_ids: int32 [32], P('adapter'), may hold values from 0 to 127
Outputs:
- served: bfloat16 [4096, 8192], P('adapter', 'feature')
All inputs are finite; a program needn't handle non-finite values.
Results may differ from a plain program's by a relative error of at most 0.025.
Values may be sent and summed in bfloat16 or wider, within the bound.
A program may use at most 64 MiB of HBM per device.

v0:
```python
import jax
import jax.numpy as jnp
from jax import lax
from jax.sharding import PartitionSpec as P

SWEEPS = 3
highest = lax.Precision.HIGHEST


def project(adapter_stack, basis_low):
    flat = adapter_stack.reshape(-1, adapter_stack.shape[-1])
    result = jnp.dot(flat, basis_low, preferred_element_type=jnp.float32)
    return result.reshape(adapter_stack.shape[0], adapter_stack.shape[1], -1)


def core_of(cols_q, rows_p):
    return jnp.einsum("irk,irl->ikl", cols_q, rows_p, precision=highest)


def numerator(adapter_stack, weighted):
    flat = adapter_stack.reshape(-1, adapter_stack.shape[-1])
    terms = weighted.reshape(-1, weighted.shape[-1])
    return lax.dot_general(
        flat, terms, (((0,), (0,)), ((), ())), preferred_element_type=jnp.float32
    )


def solve_with(gram_sum, matrix):
    factor = jnp.linalg.cholesky(gram_sum)
    return lax.linalg.triangular_solve(
        factor, matrix, left_side=False, lower=True, transpose_a=True
    )


def renew(local_term):
    full_term = lax.psum(local_term, "adapter")
    gram_sum = lax.psum(jnp.dot(full_term.T, full_term, precision=highest), "feature")
    return solve_with(gram_sum, full_term)


def down_sum(adapter_down, basis_v):
    return lax.psum(project(adapter_down, basis_v.astype(jnp.bfloat16)), "feature")


def up_sum(adapter_up, basis_u):
    return lax.psum(project(adapter_up, basis_u.astype(jnp.bfloat16)), "feature")


def on_device(adapter_down, adapter_up, fisher, init_v, init_u, prompt_rows, request_ids):
    basis_v = init_v
    basis_u = init_u
    weights = fisher[:, None, None]
    cols_q = up_sum(adapter_up, basis_u)
    for sweep_index in range(SWEEPS):
        rows_p = down_sum(adapter_down, basis_v)
        core_stack = core_of(cols_q, rows_p)
        weighted = (
            weights * jnp.einsum("irl,ikl->irk", rows_p, core_stack, precision=highest)
        ).astype(jnp.bfloat16)
        basis_u = renew(numerator(adapter_up, weighted))
        cols_q = up_sum(adapter_up, basis_u)
        core_stack = core_of(cols_q, rows_p)
        weighted = (
            weights * jnp.einsum("irk,ikl->irl", cols_q, core_stack, precision=highest)
        ).astype(jnp.bfloat16)
        basis_v = renew(numerator(adapter_down, weighted))
    rows_p = down_sum(adapter_down, basis_v)
    final_cores = core_of(cols_q, rows_p).astype(jnp.bfloat16)
    count_local = final_cores.shape[0]
    basis_width = final_cores.shape[1]
    flat_cores = final_cores.reshape(count_local, basis_width * basis_width)
    every_core = lax.all_gather(flat_cores, "adapter", axis=0, tiled=True)
    onehot = (
        request_ids[:, None] == jnp.arange(every_core.shape[0], dtype=jnp.int32)[None, :]
    ).astype(jnp.bfloat16)
    own_cores = jnp.dot(onehot, every_core, preferred_element_type=jnp.float32).astype(jnp.bfloat16)
    partial_rows = jnp.dot(
        prompt_rows, basis_v.astype(jnp.bfloat16), preferred_element_type=jnp.float32
    )
    hidden = lax.psum(partial_rows, "feature").astype(jnp.bfloat16)
    blocks = own_cores.shape[0]
    blocked = hidden.reshape(blocks, -1, basis_width)
    mixed_rows = jnp.einsum(
        "bnl,bkl->bnk",
        blocked,
        own_cores.reshape(blocks, basis_width, basis_width),
        preferred_element_type=jnp.float32,
    ).astype(jnp.bfloat16)
    served = jnp.dot(
        mixed_rows.reshape(-1, basis_width),
        basis_u.astype(jnp.bfloat16).T,
        preferred_element_type=jnp.float32,
    )
    return served.astype(jnp.bfloat16)


def solution(mesh):
    placed = (
        P("adapter", None, "feature"),
        P("adapter", None, "feature"),
        P("adapter"),
        P("feature", None),
        P("feature", None),
        P("adapter", "feature"),
        P("adapter"),
    )
    return jax.shard_map(
        on_device, mesh=mesh, in_specs=placed, out_specs=P("adapter", "feature"), check_vma=False
    )
```

profile of v0, /device:TPU:0, one launch (start us, length us, event | category | flops | bytes accessed | tf_op | source)
XLA Modules:
  0.0 935.1 jit_solution(6961525895619962585)
XLA Ops:
  11.3 35.2 %all-reduce.40.cloned.1.call-done = (f32[16,16,64]{2,1,0:T(8,128)}, f32[16,16,64]{2,1,0:T(8,128)}) async-done(((f32[16,16,64]{2,1,0:T(8,128)}, f32[16,16,64]{2,1,0:T(8,128)}), (f32[16,16,64]{2,1,0:T(8,128)}, f32[16,16,64]{2,1,0:T(8,128)})) %all-reduce.40.cloned.1.call-update) | async-done | bytes 131088 | tf_op jit(solution)/shard_map/psum | solution.py:42
  51.5 72.8 %all-reduce.16.cloned.1.call-done = f32[2048,64]{0,1:T(8,128)} async-done(((f32[2048,64]{0,1:T(8,128)}), f32[2048,64]{0,1:T(8,128)}) %all-reduce.16.cloned.1.call-update) | async-done | bytes 524304 | tf_op jit(solution)/shard_map/psum | solution.py:36
  126.1 10.3 %psum.150 = f32[64,64]{0,1:T(8,128)S(1)} all-reduce(f32[64,64]{0,1:T(8,128)S(1)} %fusion.53), channel_id=1, replica_groups=mesh['adapter'=8,'feature'=4] {'feature'}, use_global_device_ids=true, to_apply=%region_3.0 | all-reduce | flops 4096 | bytes 32768 | tf_op jit(solution)/shard_map/psum | solution.py:37
  136.4 5.8 cholesky.104
  151.5 31.2 %all-reduce.18.cloned.1.call-done = f32[16,16,64]{2,1,0:T(8,128)} async-done(((f32[16,16,64]{2,1,0:T(8,128)}), f32[16,16,64]{2,1,0:T(8,128)}) %all-reduce.18.cloned.1.call-update) | async-done | bytes 65552 | tf_op jit(solution)/shard_map/psum | solution.py:46
  188.5 72.9 %all-reduce.20.cloned.1.call-done = f32[2048,64]{0,1:T(8,128)} async-done(((f32[2048,64]{0,1:T(8,128)}), f32[2048,64]{0,1:T(8,128)}) %all-reduce.20.cloned.1.call-update) | async-done | bytes 524304 | tf_op jit(solution)/shard_map/psum | solution.py:36
  263.2 10.3 %psum.153 = f32[64,64]{0,1:T(8,128)S(1)} all-reduce(f32[64,64]{0,1:T(8,128)S(1)} %fusion.55), channel_id=1, replica_groups=mesh['adapter'=8,'feature'=4] {'feature'}, use_global_device_ids=true, to_apply=%region_8.11 | all-reduce | flops 4096 | bytes 32768 | tf_op jit(solution)/shard_map/psum | solution.py:37
  290.0 31.1 %all-reduce.22.cloned.1.call-done = f32[16,16,64]{2,1,0:T(8,128)} async-done(((f32[16,16,64]{2,1,0:T(8,128)}), f32[16,16,64]{2,1,0:T(8,128)}) %all-reduce.22.cloned.1.call-update) | async-done | bytes 65552 | tf_op jit(solution)/shard_map/psum | solution.py:42
  326.0 72.9 %all-reduce.24.cloned.1.call-done = f32[2048,64]{0,1:T(8,128)} async-done(((f32[2048,64]{0,1:T(8,128)}), f32[2048,64]{0,1:T(8,128)}) %all-reduce.24.cloned.1.call-update) | async-done | bytes 524304 | tf_op jit(solution)/shard_map/psum | solution.py:36
  400.7 10.3 %psum.156 = f32[64,64]{0,1:T(8,128)S(1)} all-reduce(f32[64,64]{0,1:T(8,128)S(1)} %fusion.57), channel_id=1, replica_groups=mesh['adapter'=8,'feature'=4] {'feature'}, use_global_device_ids=true, to_apply=%region_11.14 | all-reduce | flops 4096 | bytes 32768 | tf_op jit(solution)/shard_map/psum | solution.py:37
  426.1 31.2 %all-reduce.26.cloned.1.call-done = f32[16,16,64]{2,1,0:T(8,128)} async-done(((f32[16,16,64]{2,1,0:T(8,128)}), f32[16,16,64]{2,1,0:T(8,128)}) %all-reduce.26.cloned.1.call-update) | async-done | bytes 65552 | tf_op jit(solution)/shard_map/psum | solution.py:46
  463.1 72.9 %all-reduce.28.cloned.1.call-done = f32[2048,64]{0,1:T(8,128)} async-done(((f32[2048,64]{0,1:T(8,128)}), f32[2048,64]{0,1:T(8,128)}) %all-reduce.28.cloned.1.call-update) | async-done | bytes 524304 | tf_op jit(solution)/shard_map/psum | solution.py:36
  537.8 10.3 %psum.159 = f32[64,64]{0,1:T(8,128)S(1)} all-reduce(f32[64,64]{0,1:T(8,128)S(1)} %fusion.59), channel_id=1, replica_groups=mesh['adapter'=8,'feature'=4] {'feature'}, use_global_device_ids=true, to_apply=%region_14.17 | all-reduce | flops 4096 | bytes 32768 | tf_op jit(solution)/shard_map/psum | solution.py:37
  564.4 31.2 %all-reduce.30.cloned.1.call-done = f32[16,16,64]{2,1,0:T(8,128)} async-done(((f32[16,16,64]{2,1,0:T(8,128)}), f32[16,16,64]{2,1,0:T(8,128)}) %all-reduce.30.cloned.1.call-update) | async-done | bytes 65552 | tf_op jit(solution)/shard_map/psum | solution.py:42
  600.8 72.7 %all-reduce.32.cloned.1.call-done = f32[2048,64]{0,1:T(8,128)} async-done(((f32[2048,64]{0,1:T(8,128)}), f32[2048,64]{0,1:T(8,128)}) %all-reduce.32.cloned.1.call-update) | async-done | bytes 524304 | tf_op jit(solution)/shard_map/psum | solution.py:36
  675.2 10.3 %psum.162 = f32[64,64]{0,1:T(8,128)S(1)} all-reduce(f32[64,64]{0,1:T(8,128)S(1)} %fusion.61), channel_id=1, replica_groups=mesh['adapter'=8,'feature'=4] {'feature'}, use_global_device_ids=true, to_apply=%region_17.20 | all-reduce | flops 4096 | bytes 32768 | tf_op jit(solution)/shard_map/psum | solution.py:37
  702.8 31.2 %all-reduce.34.cloned.1.call-done = f32[16,16,64]{2,1,0:T(8,128)} async-done(((f32[16,16,64]{2,1,0:T(8,128)}), f32[16,16,64]{2,1,0:T(8,128)}) %all-reduce.34.cloned.1.call-update) | async-done | bytes 65552 | tf_op jit(solution)/shard_map/psum | solution.py:46
  738.7 72.7 %all-reduce.36.cloned.1.call-done = f32[2048,64]{0,1:T(8,128)} async-done(((f32[2048,64]{0,1:T(8,128)}), f32[2048,64]{0,1:T(8,128)}) %all-reduce.36.cloned.1.call-update) | async-done | bytes 524304 | tf_op jit(solution)/shard_map/psum | solution.py:36
  813.8 11.4 %psum.165 = f32[64,64]{0,1:T(8,128)} all-reduce(f32[64,64]{0,1:T(8,128)} %fusion.63), channel_id=1, replica_groups=mesh['adapter'=8,'feature'=4] {'feature'}, use_global_device_ids=true, to_apply=%region_20.23 | all-reduce | flops 4096 | bytes 32768 | tf_op jit(solution)/shard_map/psum | solution.py:37
  828.0 7.2 cholesky.159
  838.7 6.3 custom-call.15
  850.1 31.3 %all-reduce.38.cloned.1.call-done = f32[16,16,64]{2,1,0:T(8,128)} async-done(((f32[16,16,64]{2,1,0:T(8,128)}), f32[16,16,64]{2,1,0:T(8,128)}) %all-reduce.38.cloned.1.call-update) | async-done | bytes 65552 | tf_op jit(solution)/shard_map/psum | solution.py:42
  886.0 11.7 %all-reduce.41 = bf16[512,64]{0,1:T(8,128)(2,1)S(1)} all-reduce(f32[512,64]{0,1:T(8,128)S(1)} %convolution_bitcast_fusion.12), channel_id=1, replica_groups=mesh['adapter'=8,'feature'=4] {'feature'}, use_global_device_ids=true, to_apply=%region_21.24 | all-reduce | flops 32768 | bytes 196608 | tf_op jit(solution)/shard_map/psum | solution.py:80
  897.7 27.0 %all-gather.2.cloned.1.call-done = bf16[128,4096]{1,0:T(8,128)(2,1)} async-done(((bf16[16,4096]{1,0:T(8,128)(2,1)}), bf16[128,4096]{1,0:T(8,128)(2,1)}) %all-gather.2.cloned.1.call-update) | async-done | bytes 1048592 | tf_op jit(solution)/shard_map/all_gather | solution.py:72
  (142 shorter events, 141.4 us)
Async XLA Ops:
  6.5 877.8 %copy-start = (bf16[512,2048]{1,0:T(8,128)(2,1)S(1)}, bf16[512,2048]{1,0:T(8,128)(2,1)}, u32[]{:S(2)}) copy-start(bf16[512,2048]{1,0:T(8,128)(2,1)} %param.15) | copy-start | bytes 6291460
  6.5 41.9 %copy-start.10 = (f32[16]{0:T(128)S(1)}, f32[16]{0:T(128)}, u32[]{:S(2)}) copy-start(f32[16]{0:T(128)} %param.12) | copy-start | bytes 196
  6.5 40.0 %all-reduce.40.cloned.1.call-start = ((), (), s32[]{:S(2)}) async-start(), calls=%async_computation.13 | async-start | bytes 524288 | tf_op jit(solution)/shard_map/psum | solution.py:42
  11.3 113.0 %all-reduce.16.cloned.1.call-start = ((), (), s32[]{:S(2)}) async-start(), calls=%async_computation | async-start | bytes 1048576 | tf_op jit(solution)/shard_map/psum | solution.py:36
  51.5 131.2 %copy-start.4 = (f32[16,16,64]{2,1,0:T(8,128)S(1)}, f32[16,16,64]{2,1,0:T(8,128)}, u32[]{:S(2)}) copy-start(f32[16,16,64]{2,1,0:T(8,128)} %get-tuple-element.6) | copy-start | bytes 196612
  51.5 131.2 %all-reduce.18.cloned.1.call-start = ((), (), s32[]{:S(2)}) async-start(), calls=%async_computation.1 | async-start | bytes 262144 | tf_op jit(solution)/shard_map/psum | solution.py:46
  151.4 110.0 %all-reduce.20.cloned.1.call-start = ((), (), s32[]{:S(2)}) async-start(), calls=%async_computation.2 | async-start | bytes 1048576 | tf_op jit(solution)/shard_map/psum | solution.py:36
  188.5 132.6 %copy-start.5 = (f32[16,16,64]{2,1,0:T(8,128)S(1)}, f32[16,16,64]{2,1,0:T(8,128)}, u32[]{:S(2)}) copy-start(f32[16,16,64]{2,1,0:T(8,128)} %all-reduce.18.cloned.1.call-done) | copy-start | bytes 196612
  188.5 132.6 %all-reduce.22.cloned.1.call-start = ((), (), s32[]{:S(2)}) async-start(), calls=%async_computation.3 | async-start | bytes 262144 | tf_op jit(solution)/shard_map/psum | solution.py:42
  289.8 109.1 %all-reduce.24.cloned.1.call-start = ((), (), s32[]{:S(2)}) async-start(), calls=%async_computation.4 | async-start | bytes 1048576 | tf_op jit(solution)/shard_map/psum | solution.py:36
  325.9 131.4 %copy-start.6 = (f32[16,16,64]{2,1,0:T(8,128)S(1)}, f32[16,16,64]{2,1,0:T(8,128)}, u32[]{:S(2)}) copy-start(f32[16,16,64]{2,1,0:T(8,128)} %all-reduce.22.cloned.1.call-done) | copy-start | bytes 196612
  325.9 131.3 %all-reduce.26.cloned.1.call-start = ((), (), s32[]{:S(2)}) async-start(), calls=%async_computation.5 | async-start | bytes 262144 | tf_op jit(solution)/shard_map/psum | solution.py:46
  426.0 110.0 %all-reduce.28.cloned.1.call-start = ((), (), s32[]{:S(2)}) async-start(), calls=%async_computation.6 | async-start | bytes 1048576 | tf_op jit(solution)/shard_map/psum | solution.py:36
  463.1 132.6 %copy-start.7 = (f32[16,16,64]{2,1,0:T(8,128)S(1)}, f32[16,16,64]{2,1,0:T(8,128)}, u32[]{:S(2)}) copy-start(f32[16,16,64]{2,1,0:T(8,128)} %all-reduce.26.cloned.1.call-done) | copy-start | bytes 196612
  463.1 132.6 %all-reduce.30.cloned.1.call-start = ((), (), s32[]{:S(2)}) async-start(), calls=%async_computation.7 | async-start | bytes 262144 | tf_op jit(solution)/shard_map/psum | solution.py:42
  564.4 109.1 %all-reduce.32.cloned.1.call-start = ((), (), s32[]{:S(2)}) async-start(), calls=%async_computation.8 | async-start | bytes 1048576 | tf_op jit(solution)/shard_map/psum | solution.py:36
  600.5 133.5 %copy-start.8 = (f32[16,16,64]{2,1,0:T(8,128)S(1)}, f32[16,16,64]{2,1,0:T(8,128)}, u32[]{:S(2)}) copy-start(f32[16,16,64]{2,1,0:T(8,128)} %all-reduce.30.cloned.1.call-done) | copy-start | bytes 196612
  600.5 133.5 %all-reduce.34.cloned.1.call-start = ((), (), s32[]{:S(2)}) async-start(), calls=%async_computation.9 | async-start | bytes 262144 | tf_op jit(solution)/shard_map/psum | solution.py:46
  701.1 36.4 %copy-start.2 = (bf16[16,16,2048]{2,1,0:T(8,128)(2,1)S(1)}, bf16[16,16,2048]{2,1,0:T(8,128)(2,1)}, u32[]{:S(2)}) copy-start(bf16[16,16,2048]{2,1,0:T(8,128)(2,1)} %param.10) | copy-start | bytes 3145732
  702.8 108.6 %all-reduce.36.cloned.1.call-start = ((), (), s32[]{:S(2)}) async-start(), calls=%async_computation.10 | async-start | bytes 1048576 | tf_op jit(solution)/shard_map/psum | solution.py:36
  738.6 142.8 %copy-start.9 = (f32[16,16,64]{2,1,0:T(8,128)S(1)}, f32[16,16,64]{2,1,0:T(8,128)}, u32[]{:S(2)}) copy-start(f32[16,16,64]{2,1,0:T(8,128)} %all-reduce.34.cloned.1.call-done) | copy-start | bytes 196612
  738.6 142.8 %all-reduce.38.cloned.1.call-start = ((), (), s32[]{:S(2)}) async-start(), calls=%async_computation.11 | async-start | bytes 262144 | tf_op jit(solution)/shard_map/psum | solution.py:42
  848.4 76.3 %copy-start.11 = (s32[4]{0:T(128)S(1)}, s32[4]{0:T(128)}, u32[]{:S(2)}) copy-start(s32[4]{0:T(128)} %param.16) | copy-start | bytes 52
  850.0 74.7 %all-gather.2.cloned.1.call-start = ((), (), s32[]{:S(2)}) async-start(), calls=%async_computation.12 | async-start | bytes 1179648 | tf_op jit(solution)/shard_map/all_gather | solution.py:72
  (2 other events, 3.3 us)
Sparse Core Ops, SparseCore 0:
  11.4 35.0 all-reduce.39
  51.6 72.6 all-reduce.15
  151.5 31.1 all-reduce.17
  188.6 72.7 all-reduce.19
  289.9 31.1 all-reduce.21
  326.1 72.7 all-reduce.23
  426.1 31.1 all-reduce.25
  463.2 72.7 all-reduce.27
  564.5 31.1 all-reduce.29
  600.6 72.7 all-reduce.31
  702.9 31.1 all-reduce.33
  738.7 72.6 all-reduce.35
  850.2 31.2 all-reduce.37
  884.4 40.2 all-gather.1
where the time goes:
time: 937 us; the launch traced here: 935 us
  waiting for transfers between devices  686 us (73%)
  other arithmetic  79.4 us (8%)
  blocking collectives  74.4 us (8%)
  matrix products  70.3 us (8%)
  between operations  13.7 us (1%)
  local copies, waits for them, and re-layouts  9.93 us (1%)
    psum x6, waiting for transfers between devices, renew(): full_term = lax.psum(local_term, 'adapter')  437 us
    psum x4, waiting for transfers between devices, down_sum(): lax.psum(project(adapter_down, basis_v.astype(jnp.bfloat16)), 'feature')  129 us
    psum x3, waiting for transfers between devices, up_sum(): lax.psum(project(adapter_up, basis_u.astype(jnp.bfloat16)), 'feature')  93.7 us
    psum x6, blocking collectives, renew(): lax.psum(jnp.dot(full_term.T, full_term, precision=highest), 'feature')  62.7 us
    another operation x18, other arithmetic, solve_with(): factor = jnp.linalg.cholesky(gram_sum)  41.3 us
    another operation x12, other arithmetic, solve_with(): lax.linalg.triangular_solve(factor, matrix, left_side=False, lower=True,...  36.7 us
    all_gather x1, waiting for transfers between devices, on_device(): every_core = lax.all_gather(flat_cores, 'adapter', axis=0, tiled=True)  27 us
  transfers between devices with their start and end apart: 14, of which 14 were waited for; matrix products, arithmetic and copies ran while one was open for 0% of the time, Pallas kernels for 0%

commit v1 on v0

--- a/solution.py
+++ b/solution.py
@@ -39,7 +39,9 @@
 
 
 def down_sum(adapter_down, basis_v):
-    return lax.psum(project(adapter_down, basis_v.astype(jnp.bfloat16)), "feature")
+    return jnp.sum(
+        lax.all_gather(project(adapter_down, basis_v.astype(jnp.bfloat16)), "feature"), axis=0
+    )
 
 
 def up_sum(adapter_up, basis_u):

time: 937 us -> 855 us (0.912)
  waiting for transfers between devices: 686 us -> 576 us
  blocking collectives: 74.4 us -> 108 us
    psum x4 -> x0, waiting for transfers between devices: 129 us -> none  [down_sum(): lax.psum(project(adapter_down, basis_v.astype(jnp.bfloat16)), 'feature')]
    all_gather x0 -> x4, blocking collectives: none -> 32.7 us  [down_sum(): lax.all_gather(project(adapter_down, basis_v.astype(jnp.bfloat16)), 'feat...]
    psum x3 -> x4, waiting for transfers between devices: 93.7 us -> 117 us  [up_sum(): lax.psum(project(adapter_up, basis_u.astype(jnp.bfloat16)), 'feature')]
  transfers between devices with their start and end apart: 14 -> 11, of which waited for: 14 -> 11; matrix products, arithmetic and copies ran while one was open for 0% -> 0% of each run, Pallas kernels for 0% -> 0%
where the time goes in v1:
time: 855 us; the launch traced here: 853 us
  waiting for transfers between devices  576 us (67%)
  blocking collectives  108 us (13%)
  other arithmetic  82.7 us (10%)
  matrix products  63.6 us (7%)
  between operations  13.7 us (2%)
    psum x6, waiting for transfers between devices, renew(): full_term = lax.psum(local_term, 'adapter')  434 us
    psum x4, waiting for transfers between devices, up_sum(): lax.psum(project(adapter_up, basis_u.astype(jnp.bfloat16)), 'feature')  117 us
    psum x6, blocking collectives, renew(): lax.psum(jnp.dot(full_term.T, full_term, precision=highest), 'feature')  63.1 us
    another operation x18, other arithmetic, solve_with(): factor = jnp.linalg.cholesky(gram_sum)  41.3 us
    another operation x12, other arithmetic, solve_with(): lax.linalg.triangular_solve(factor, matrix, left_side=False, lower=True,...  36.7 us
    all_gather x4, blocking collectives, down_sum(): lax.all_gather(project(adapter_down, basis_v.astype(jnp.bfloat16)), 'feat...  32.7 us
    all_gather x1, waiting for transfers between devices, on_device(): every_core = lax.all_gather(flat_cores, 'adapter', axis=0, tiled=True)  25.5 us
  transfers between devices with their start and end apart: 11, of which 11 were waited for; matrix products, arithmetic and copies ran while one was open for 0% of the time, Pallas kernels for 0%

profile of v1, /device:TPU:0, one launch (start us, length us, event | category | flops | bytes accessed | tf_op | source)
XLA Modules:
  0.0 853.2 jit_solution(13234210544477942177)
XLA Ops:
  11.1 9.1 %all-gather = f32[64,16,64]{2,1,0:T(8,128)} all-gather(f32[16,16,64]{2,1,0:T(8,128)S(1)} %fusion.15), channel_id=2, replica_groups=mesh['adapter'=8,'feature'=4] {'feature'}, dimensions={0}, use_global_device_ids=true | all-gather | bytes 327680 | tf_op jit(solution)/shard_map/all_gather | solution.py:43
  21.3 22.9 %all-reduce.12.cloned.1.call-done = f32[16,16,64]{2,1,0:T(8,128)} async-done(((f32[16,16,64]{2,1,0:T(8,128)}), f32[16,16,64]{2,1,0:T(8,128)}) %all-reduce.12.cloned.1.call-update) | async-done | bytes 65552 | tf_op jit(solution)/shard_map/psum | solution.py:48
  48.2 72.9 %all-reduce.14.cloned.1.call-done = f32[2048,64]{0,1:T(8,128)} async-done(((f32[2048,64]{0,1:T(8,128)}), f32[2048,64]{0,1:T(8,128)}) %all-reduce.14.cloned.1.call-update) | async-done | bytes 524304 | tf_op jit(solution)/shard_map/psum | solution.py:36
  122.9 10.3 %psum.121 = f32[64,64]{0,1:T(8,128)S(1)} all-reduce(f32[64,64]{0,1:T(8,128)S(1)} %fusion.53), channel_id=1, replica_groups=mesh['adapter'=8,'feature'=4] {'feature'}, use_global_device_ids=true, to_apply=%region_3.0 | all-reduce | flops 4096 | bytes 32768 | tf_op jit(solution)/shard_map/psum | solution.py:37
  148.3 31.2 %all-reduce.16.cloned.1.call-done = f32[16,16,64]{2,1,0:T(8,128)} async-done(((f32[16,16,64]{2,1,0:T(8,128)}), f32[16,16,64]{2,1,0:T(8,128)}) %all-reduce.16.cloned.1.call-update) | async-done | bytes 65552 | tf_op jit(solution)/shard_map/psum | solution.py:48
  185.3 72.7 %all-reduce.18.cloned.1.call-done = f32[2048,64]{0,1:T(8,128)} async-done(((f32[2048,64]{0,1:T(8,128)}), f32[2048,64]{0,1:T(8,128)}) %all-reduce.18.cloned.1.call-update) | async-done | bytes 524304 | tf_op jit(solution)/shard_map/psum | solution.py:36
  259.9 10.4 %psum.124 = f32[64,64]{0,1:T(8,128)S(1)} all-reduce(f32[64,64]{0,1:T(8,128)S(1)} %fusion.55), channel_id=1, replica_groups=mesh['adapter'=8,'feature'=4] {'feature'}, use_global_device_ids=true, to_apply=%region_8.11 | all-reduce | flops 4096 | bytes 32768 | tf_op jit(solution)/shard_map/psum | solution.py:37
  285.9 7.9 all_gather.16
  298.1 71.4 %all-reduce.20.cloned.1.call-done = f32[2048,64]{0,1:T(8,128)} async-done(((f32[2048,64]{0,1:T(8,128)}), f32[2048,64]{0,1:T(8,128)}) %all-reduce.20.cloned.1.call-update) | async-done | bytes 524304 | tf_op jit(solution)/shard_map/psum | solution.py:36
  371.3 10.3 %psum.126 = f32[64,64]{0,1:T(8,128)S(1)} all-reduce(f32[64,64]{0,1:T(8,128)S(1)} %fusion.57), channel_id=1, replica_groups=mesh['adapter'=8,'feature'=4] {'feature'}, use_global_device_ids=true, to_apply=%region_11.14 | all-reduce | flops 4096 | bytes 32768 | tf_op jit(solution)/shard_map/psum | solution.py:37
  396.7 31.2 %all-reduce.22.cloned.1.call-done = f32[16,16,64]{2,1,0:T(8,128)} async-done(((f32[16,16,64]{2,1,0:T(8,128)}), f32[16,16,64]{2,1,0:T(8,128)}) %all-reduce.22.cloned.1.call-update) | async-done | bytes 65552 | tf_op jit(solution)/shard_map/psum | solution.py:48
  433.7 72.9 %all-reduce.24.cloned.1.call-done = f32[2048,64]{0,1:T(8,128)} async-done(((f32[2048,64]{0,1:T(8,128)}), f32[2048,64]{0,1:T(8,128)}) %all-reduce.24.cloned.1.call-update) | async-done | bytes 524304 | tf_op jit(solution)/shard_map/psum | solution.py:36
  508.4 10.4 %psum.129 = f32[64,64]{0,1:T(8,128)S(1)} all-reduce(f32[64,64]{0,1:T(8,128)S(1)} %fusion.59), channel_id=1, replica_groups=mesh['adapter'=8,'feature'=4] {'feature'}, use_global_device_ids=true, to_apply=%region_14.17 | all-reduce | flops 4096 | bytes 32768 | tf_op jit(solution)/shard_map/psum | solution.py:37
  534.5 8.0 all_gather.17
  546.7 71.4 %all-reduce.26.cloned.1.call-done = f32[2048,64]{0,1:T(8,128)} async-done(((f32[2048,64]{0,1:T(8,128)}), f32[2048,64]{0,1:T(8,128)}) %all-reduce.26.cloned.1.call-update) | async-done | bytes 524304 | tf_op jit(solution)/shard_map/psum | solution.py:36
  619.9 10.3 %psum.131 = f32[64,64]{0,1:T(8,128)S(1)} all-reduce(f32[64,64]{0,1:T(8,128)S(1)} %fusion.61), channel_id=1, replica_groups=mesh['adapter'=8,'feature'=4] {'feature'}, use_global_device_ids=true, to_apply=%region_17.20 | all-reduce | flops 4096 | bytes 32768 | tf_op jit(solution)/shard_map/psum | solution.py:37
  647.5 31.2 %all-reduce.28.cloned.1.call-done = f32[16,16,64]{2,1,0:T(8,128)} async-done(((f32[16,16,64]{2,1,0:T(8,128)}), f32[16,16,64]{2,1,0:T(8,128)}) %all-reduce.28.cloned.1.call-update) | async-done | bytes 65552 | tf_op jit(solution)/shard_map/psum | solution.py:48
  683.3 72.7 %all-reduce.30.cloned.1.call-done = f32[2048,64]{0,1:T(8,128)} async-done(((f32[2048,64]{0,1:T(8,128)}), f32[2048,64]{0,1:T(8,128)}) %all-reduce.30.cloned.1.call-update) | async-done | bytes 524304 | tf_op jit(solution)/shard_map/psum | solution.py:36
  758.4 11.5 %psum.134 = f32[64,64]{0,1:T(8,128)} all-reduce(f32[64,64]{0,1:T(8,128)} %fusion.63), channel_id=1, replica_groups=mesh['adapter'=8,'feature'=4] {'feature'}, use_global_device_ids=true, to_apply=%region_20.23 | all-reduce | flops 4096 | bytes 32768 | tf_op jit(solution)/shard_map/psum | solution.py:37
  772.8 7.2 cholesky.159
  783.5 6.3 custom-call.15
  794.2 7.7 all_gather.18
  804.7 12.6 %all-reduce.31 = bf16[512,64]{0,1:T(8,128)(2,1)S(1)} all-reduce(f32[512,64]{0,1:T(8,128)S(1)} %convolution_bitcast_fusion.12), channel_id=1, replica_groups=mesh['adapter'=8,'feature'=4] {'feature'}, use_global_device_ids=true, to_apply=%region_21.24 | all-reduce | flops 32768 | bytes 196608 | tf_op jit(solution)/shard_map/psum | solution.py:82
  817.3 25.5 %all-gather.3.cloned.1.call-done = bf16[128,4096]{1,0:T(8,128)(2,1)} async-done(((bf16[16,4096]{1,0:T(8,128)(2,1)}), bf16[128,4096]{1,0:T(8,128)(2,1)}) %all-gather.3.cloned.1.call-update) | async-done | bytes 1048592 | tf_op jit(solution)/shard_map/all_gather | solution.py:74
  (137 shorter events, 141.3 us)
Async XLA Ops:
  6.5 797.4 %copy-start = (bf16[512,2048]{1,0:T(8,128)(2,1)S(1)}, bf16[512,2048]{1,0:T(8,128)(2,1)}, u32[]{:S(2)}) copy-start(bf16[512,2048]{1,0:T(8,128)(2,1)} %param.15) | copy-start | bytes 6291460
  6.5 37.7 %all-reduce.12.cloned.1.call-start = ((), (), s32[]{:S(2)}) async-start(), calls=%async_computation | async-start | bytes 262144 | tf_op jit(solution)/shard_map/psum | solution.py:48
  9.1 37.0 %copy-start.8 = (f32[16]{0:T(128)S(1)}, f32[16]{0:T(128)}, u32[]{:S(2)}) copy-start(f32[16]{0:T(128)} %param.12) | copy-start | bytes 196
  9.2 37.9 %copy-start.1 = (bf16[16,16,2048]{2,1,0:T(8,128)(2,1)S(1)}, bf16[16,16,2048]{2,1,0:T(8,128)(2,1)}, u32[]{:S(2)}) copy-start(bf16[16,16,2048]{2,1,0:T(8,128)(2,1)} %param.11) | copy-start | bytes 3145732
  9.2 112.0 %all-reduce.14.cloned.1.call-start = ((), (), s32[]{:S(2)}) async-start(), calls=%async_computation.1 | async-start | bytes 1048576 | tf_op jit(solution)/shard_map/psum | solution.py:36
  48.2 131.4 %all-reduce.16.cloned.1.call-start = ((), (), s32[]{:S(2)}) async-start(), calls=%async_computation.2 | async-start | bytes 262144 | tf_op jit(solution)/shard_map/psum | solution.py:48
  148.3 109.8 %all-reduce.18.cloned.1.call-start = ((), (), s32[]{:S(2)}) async-start(), calls=%async_computation.3 | async-start | bytes 1048576 | tf_op jit(solution)/shard_map/psum | solution.py:36
  185.3 184.2 %all-reduce.20.cloned.1.call-start = ((), (), s32[]{:S(2)}) async-start(), calls=%async_computation.4 | async-start | bytes 1048576 | tf_op jit(solution)/shard_map/psum | solution.py:36
  259.9 35.1 %copy-start.5 = (f32[16,16,64]{2,1,0:T(8,128)S(1)}, f32[16,16,64]{2,1,0:T(8,128)}, u32[]{:S(2)}) copy-start(f32[16,16,64]{2,1,0:T(8,128)} %all-reduce.16.cloned.1.call-done) | copy-start | bytes 196612
  298.0 129.9 %all-reduce.22.cloned.1.call-start = ((), (), s32[]{:S(2)}) async-start(), calls=%async_computation.5 | async-start | bytes 262144 | tf_op jit(solution)/shard_map/psum | solution.py:48
  396.6 110.0 %all-reduce.24.cloned.1.call-start = ((), (), s32[]{:S(2)}) async-start(), calls=%async_computation.6 | async-start | bytes 1048576 | tf_op jit(solution)/shard_map/psum | solution.py:36
  433.7 184.4 %all-reduce.26.cloned.1.call-start = ((), (), s32[]{:S(2)}) async-start(), calls=%async_computation.7 | async-start | bytes 1048576 | tf_op jit(solution)/shard_map/psum | solution.py:36
  508.4 35.1 %copy-start.6 = (f32[16,16,64]{2,1,0:T(8,128)S(1)}, f32[16,16,64]{2,1,0:T(8,128)}, u32[]{:S(2)}) copy-start(f32[16,16,64]{2,1,0:T(8,128)} %all-reduce.22.cloned.1.call-done) | copy-start | bytes 196612
  546.6 132.1 %all-reduce.28.cloned.1.call-start = ((), (), s32[]{:S(2)}) async-start(), calls=%async_computation.8 | async-start | bytes 262144 | tf_op jit(solution)/shard_map/psum | solution.py:48
  645.7 36.4 %copy-start.2 = (bf16[16,16,2048]{2,1,0:T(8,128)(2,1)S(1)}, bf16[16,16,2048]{2,1,0:T(8,128)(2,1)}, u32[]{:S(2)}) copy-start(bf16[16,16,2048]{2,1,0:T(8,128)(2,1)} %param.10) | copy-start | bytes 3145732
  647.4 108.6 %all-reduce.30.cloned.1.call-start = ((), (), s32[]{:S(2)}) async-start(), calls=%async_computation.9 | async-start | bytes 1048576 | tf_op jit(solution)/shard_map/psum | solution.py:36
  683.2 159.6 %all-gather.3.cloned.1.call-start = ((), (), s32[]{:S(2)}) async-start(), calls=%async_computation.10 | async-start | bytes 1179648 | tf_op jit(solution)/shard_map/all_gather | solution.py:74
  758.4 43.5 %copy-start.7 = (f32[16,16,64]{2,1,0:T(8,128)S(1)}, f32[16,16,64]{2,1,0:T(8,128)}, u32[]{:S(2)}) copy-start(f32[16,16,64]{2,1,0:T(8,128)} %all-reduce.28.cloned.1.call-done) | copy-start | bytes 196612
  791.4 0.7 copy-start.3
  793.2 10.7 %copy-start.4 = (bf16[2048,64]{0,1:T(8,128)(2,1)S(1)}, bf16[2048,64]{0,1:T(8,128)(2,1)}, u32[]{:S(2)}) copy-start(bf16[2048,64]{0,1:T(8,128)(2,1)} %copy-done.3) | copy-start | bytes 786436
  801.9 41.0 %copy-start.9 = (s32[4]{0:T(128)S(1)}, s32[4]{0:T(128)}, u32[]{:S(2)}) copy-start(s32[4]{0:T(128)} %param.16) | copy-start | bytes 52
Sparse Core Ops, SparseCore 0:
  9.6 34.4 all-reduce.11
  48.3 72.7 all-reduce.13
  148.4 31.1 all-reduce.15
  185.4 72.6 all-reduce.17
  298.2 71.3 all-reduce.19
  396.8 31.1 all-reduce.21
  433.8 72.7 all-reduce.23
  546.7 71.3 all-reduce.25
  647.5 31.1 all-reduce.27
  683.4 72.6 all-reduce.29
  804.0 38.8 all-gather.2
